TPU v7x, 128 devices: a whole 4x4x4 slice. The times are simulated.
128 devices in a mesh: ctx: 32 (over x, z, core), head: 4 (over y).
Axes of the slice: x: 4, y: 4, z: 4, core: 2. Of those that a mesh axis runs over, the one named last changes fastest.
Arguments:
- hidden_in: bfloat16 [16384, 7168], P('ctx', 'head'), may hold values from -6 to 6
- gate_weight: bfloat16 [7168, 192], P('head'), may hold values from -0.09375 to 0.09375
- encoded_queries: bfloat16 [16384, 64, 128], P('ctx', 'head'), may hold values from -12 to 12
- encoded_keys: bfloat16 [16384, 4, 128], P('ctx', 'head'), may hold values from -12 to 12
- value_tensor: bfloat16 [16384, 4, 128], P('ctx', 'head'), may hold values from -6 to 6
- comp_key_weight: float32 [64, 128], replicated, may hold values from -0.75 to 0.75
- comp_value_weight: float32 [64, 128], replicated, may hold values from -0.75 to 0.75
- selection: int32 [256, 4, 16], P('ctx', 'head'), may hold values from 0 to 255, as said below
Outputs:
- attended: bfloat16 [16384, 64, 128], P('ctx', 'head')
Inputs may be any that keep to these rules, and one draw needn't show every extreme that they name: `selection`: entries of one list are distinct and the first is the query block's own block. For one index of ctx and one group, the blocks named over all its query blocks that lie in one other index's shard are at most 4, and some index reaches 4 in every draw.
All inputs are finite; a program needn't handle non-finite values.
Results may differ from a plain program's by a relative error of at most 0.011.
Values may be sent and summed in bfloat16 or wider, within the bound.
No kernel may reach another device: no remote copies, remote signals or barrier semaphores. Data moves between devices by JAX's collectives and lax.ppermute only.
A program may use at most 64 MiB of HBM per device.

v0:
```python
import jax
import jax.numpy as jnp
from jax import lax
from jax.sharding import PartitionSpec as P

WINDOW_TOKENS = 512


def shifted(value, axis, steps):
    count = lax.axis_size(axis)
    initial, last = (max(0, -steps), min(count, count - steps))
    return lax.ppermute(value, axis, [(source, source + steps) for source in range(initial, last)])


def attend(query_block_index, key_rows, value_rows, key_mask, with_null):
    scale = query_block_index.shape[-1] ** (-0.5)
    if key_rows.dtype == jnp.float32:
        scores = (
            jnp.einsum(
                "tgjd,gkd->tgjk",
                query_block_index.astype(jnp.float32),
                key_rows,
                preferred_element_type=jnp.float32,
                precision=lax.Precision.HIGHEST,
            )
            * scale
        )
    else:
        scores = (
            jnp.einsum(
                "tgjd,gkd->tgjk", query_block_index, key_rows, preferred_element_type=jnp.float32
            )
            * scale
        )
    scores = jnp.where(key_mask[:, :, None, :], scores, -1e30)
    peak = jnp.max(scores, axis=-1, keepdims=True)
    if with_null:
        peak = jnp.maximum(peak, 0.0)
    weights = jnp.exp(scores - peak)
    total_w = jnp.sum(weights, axis=-1, keepdims=True)
    if with_null:
        total_w = total_w + jnp.exp(-peak)
    rounded = (weights / total_w).astype(jnp.bfloat16)
    if value_rows.dtype == jnp.float32:
        return jnp.einsum(
            "tgjk,gkd->tgjd",
            rounded.astype(jnp.float32),
            value_rows,
            preferred_element_type=jnp.float32,
            precision=lax.Precision.HIGHEST,
        )
    return jnp.einsum("tgjk,gkd->tgjd", rounded, value_rows, preferred_element_type=jnp.float32)


def body(
    hidden_in,
    gate_weight,
    encoded_queries,
    encoded_keys,
    value_tensor,
    comp_key_weight,
    comp_value_weight,
    selection,
):
    rows_here, heads_here, head_dim = encoded_queries.shape
    block_len = comp_key_weight.shape[0]
    top_count = selection.shape[-1]
    blocks_here = rows_here // block_len
    shard_parts = lax.axis_size("ctx")
    own_index = lax.axis_index("ctx")
    block_count_total = blocks_here * shard_parts
    window_len = WINDOW_TOKENS
    partial_value = jnp.dot(hidden_in, gate_weight, preferred_element_type=jnp.float32)
    logits = lax.psum_scatter(partial_value, "head", scatter_dimension=1, tiled=True)
    gate_values = jax.nn.sigmoid(logits).reshape(rows_here, 1, heads_here, 3)
    key_value = jnp.concatenate([encoded_keys, value_tensor], axis=-1).reshape(
        rows_here, 2 * head_dim
    )
    widened = key_value.astype(jnp.float32).reshape(blocks_here, block_len, 2 * head_dim)
    compress_w = jnp.concatenate([comp_key_weight, comp_value_weight], axis=-1)
    summary = jnp.sum(widened * compress_w[None, :, :], axis=1)
    summaries = lax.all_gather(summary, "ctx", axis=0, tiled=True)
    previous = shifted(key_value, "ctx", 1)
    extended = jnp.concatenate([previous, key_value], axis=0)
    blocks = key_value.reshape(blocks_here, block_len, 2 * head_dim)
    chosen_blocks = selection[:, 0, :]
    all_ids = jnp.arange(block_count_total, dtype=jnp.int32)
    all_blocks = lax.all_gather(blocks, "ctx", axis=0, tiled=True)
    picked = jnp.take(all_blocks, chosen_blocks, axis=0)
    offset = own_index * rows_here
    comp_ends = (all_ids + 1) * block_len - 1
    inner_result = jnp.arange(block_len, dtype=jnp.int32)
    comp_keys = summaries[None, :, :head_dim]
    comp_values = summaries[None, :, head_dim:]

    def per_block(block_num):
        query_start = block_num * block_len
        query_block_index = lax.dynamic_slice_in_dim(
            encoded_queries, query_start, block_len, 0
        ).reshape(block_len, 1, heads_here, head_dim)
        query_pos = offset + query_start + inner_result
        comp_mask = (comp_ends[None, :] <= query_pos[:, None])[:, None, :]
        out_comp = attend(query_block_index, comp_keys, comp_values, comp_mask, True)
        sel_tiles = lax.dynamic_index_in_dim(picked, block_num, 0, keepdims=False).reshape(
            top_count * block_len, 2 * head_dim
        )
        sel_ids = lax.dynamic_index_in_dim(chosen_blocks, block_num, 0, keepdims=False)
        selected_positions = (sel_ids[:, None] * block_len + inner_result[None, :]).reshape(-1)
        sel_mask = (selected_positions[None, :] <= query_pos[:, None])[:, None, :]
        out_sel = attend(
            query_block_index,
            sel_tiles[None, :, :head_dim],
            sel_tiles[None, :, head_dim:],
            sel_mask,
            False,
        )
        win_rows = lax.dynamic_slice_in_dim(extended, query_start, window_len + block_len, 0)
        win_pos = (
            offset + query_start - window_len + jnp.arange(window_len + block_len, dtype=jnp.int32)
        )
        win_mask = (
            (win_pos[None, :] <= query_pos[:, None])
            & (win_pos[None, :] > query_pos[:, None] - window_len)
            & (win_pos[None, :] >= 0)
        )
        out_win = attend(
            query_block_index,
            win_rows[None, :, :head_dim],
            win_rows[None, :, head_dim:],
            win_mask[:, None, :],
            False,
        )
        gate_block_rows = lax.dynamic_slice_in_dim(gate_values, query_start, block_len, 0)
        merged = (
            gate_block_rows[..., 0:1] * out_comp
            + gate_block_rows[..., 1:2] * out_sel
            + gate_block_rows[..., 2:3] * out_win
        )
        return merged.reshape(block_len, heads_here, head_dim).astype(jnp.bfloat16)

    results = lax.map(per_block, jnp.arange(blocks_here, dtype=jnp.int32))
    return results.reshape(rows_here, heads_here, head_dim)


def solution(mesh):
    return jax.shard_map(
        body,
        mesh=mesh,
        in_specs=(
            P("ctx", "head"),
            P("head", None),
            P("ctx", "head", None),
            P("ctx", "head", None),
            P("ctx", "head", None),
            P(),
            P(),
            P("ctx", "head", None),
        ),
        out_specs=P("ctx", "head", None),
        check_vma=False,
    )
```

profile of v0, /device:TPU:1, one launch (start us, length us, event | category | flops | bytes accessed | tf_op | source)
XLA Modules:
  0.0 289.9 jit_solution(7371172152859489917)
XLA Ops:
  7.4 1.4 copy-done
  8.9 2.6 fusion.55
  12.4 4.9 %collective-permute-start = (bf16[512,256]{1,0:T(8,128)(2,1)}, bf16[512,256]{1,0:T(8,128)(2,1)S(1)}, u32[]{:S(2)}, u32[]{:S(2)}) collective-permute-start(bf16[512,256]{1,0:T(8,128)(2,1)} %bitcast.175), channel_id=1, source_target_pairs={{0,4},{4,8},{8,12},{12,16},{16,20},{20,24},{24,28},{28,32},{32,36}... | collective-permute-start | bytes 786440 | tf_op jit(solution)/shard_map/ppermute | solution.py:12
  18.5 24.4 %all_gather.6 = f32[256,256]{1,0:T(8,128)S(1)} all-gather(f32[8,256]{1,0:T(8,128)S(1)} %multiply_reduce_fusion), channel_id=1, replica_groups=mesh['ctx'=32,'head'=4] {'ctx'}, dimensions={0}, use_global_device_ids=true | all-gather | bytes 270336 | tf_op jit(solution)/shard_map/all_gather | solution.py:82
  43.7 1.8 pad_maximum_fusion
  47.2 24.0 %all-gather.2.cloned.1.call-done = bf16[256,64,256]{2,1,0:T(8,128)(2,1)} async-done(((bf16[8,64,256]{2,1,0:T(8,128)(2,1)}), bf16[256,64,256]{2,1,0:T(8,128)(2,1)}) %all-gather.2.cloned.1.call-update) | async-done | bytes 8388624 | tf_op jit(solution)/shard_map/all_gather | solution.py:88
  71.2 6.2 %gather_fusion = bf16[128,64,256]{2,1,0:T(8,128)(2,1)} fusion(bf16[256,64,256]{2,1,0:T(8,128)(2,1)} %all-gather.2.cloned.1.call-done, s32[1024]{0:T(1024)S(1)} %pad_clamp_fusion), kind=kCustom, calls=%fused_computation | custom fusion | bytes 8389120 | tf_op jit(solution)/shard_map/jit(_take)/gather | solution.py:89
  77.4 4.6 %broadcast_select_fusion = bf16[8,16,64,256]{3,2,1,0:T(8,128)(2,1)} fusion(bf16[8,16,64,256]{3,2,1,0:T(8,128)(2,1)} %bitcast.173, pred[8,16]{1,0:T(8,128)(4,1)S(1)} %compare_and_fusion), kind=kLoop, calls=%fused_computation.68 | loop fusion | flops 2097152 | bytes 8388736 | tf_op jit(solution)/shard_map/jit(_take)/select_n | solution.py:89
  81.9 200.5 %while.15 = (s32[]{:T(128)}, bf16[8,64,16,128]{3,2,1,0:T(8,128)(2,1)}, s32[8]{0:T(128)S(1)}, f32[512,1,16,3]{0,3,2,1:T(4,128)}, s32[]{:T(128)}, /*index=5*/bf16[...) while((s32[]{:T(128)}, ...), condition=%wide.region_9.10_spmd.clone.clone, body=%wide.region_2.9_spmd.clone.clone.sunk | while | flops 1666942592 | bytes 35800808 | solution.py:141
  88.2 1.1 fusion.83
  89.3 2.1 fusion.84
  92.5 3.7 %fusion.85 = f32[1,128,64,16]{1,3,2,0:T(8,128)} fusion(bf16[64,16,1024]{2,0,1:T(8,128)(2,1)} %fusion.84, bf16[1024,256]{1,0:T(8,128)(2,1)S(1)} %bitcast.172, f32[64,16]{1,0:T(8,128)S(1)} %bitcast.180), kind=kOutput, calls=%fused_computation.23.clone.1 | convolution fusion | flops 268566528 | bytes 2916352 | tf_op jit(solution)/shard_map/while/body/eval_jaxpr/tgjk,gkd->tgjd/dot_general | solution.py:52
  96.2 1.6 fusion.86
  98.3 2.7 fusion.88
  101.1 1.6 fusion.89
  104.2 2.8 fusion.92
  113.3 1.1 fusion.83
  114.4 2.1 fusion.84
  117.5 3.7 %fusion.85 = f32[1,128,64,16]{1,3,2,0:T(8,128)} fusion(bf16[64,16,1024]{2,0,1:T(8,128)(2,1)} %fusion.84, bf16[1024,256]{1,0:T(8,128)(2,1)S(1)} %bitcast.172, f32[64,16]{1,0:T(8,128)S(1)} %bitcast.180), kind=kOutput, calls=%fused_computation.23.clone.1 | convolution fusion | flops 268566528 | bytes 2916352 | tf_op jit(solution)/shard_map/while/body/eval_jaxpr/tgjk,gkd->tgjd/dot_general | solution.py:52
  121.3 1.6 fusion.86
  123.4 2.7 fusion.88
  126.2 1.6 fusion.89
  129.3 2.8 fusion.92
  138.4 1.1 fusion.83
  139.4 2.1 fusion.84
  142.6 3.7 %fusion.85 = f32[1,128,64,16]{1,3,2,0:T(8,128)} fusion(bf16[64,16,1024]{2,0,1:T(8,128)(2,1)} %fusion.84, bf16[1024,256]{1,0:T(8,128)(2,1)S(1)} %bitcast.172, f32[64,16]{1,0:T(8,128)S(1)} %bitcast.180), kind=kOutput, calls=%fused_computation.23.clone.1 | convolution fusion | flops 268566528 | bytes 2916352 | tf_op jit(solution)/shard_map/while/body/eval_jaxpr/tgjk,gkd->tgjd/dot_general | solution.py:52
  146.4 1.6 fusion.86
  148.4 2.7 fusion.88
  151.2 1.6 fusion.89
  154.4 2.8 fusion.92
  163.4 1.1 fusion.83
  164.5 2.1 fusion.84
  167.7 3.7 %fusion.85 = f32[1,128,64,16]{1,3,2,0:T(8,128)} fusion(bf16[64,16,1024]{2,0,1:T(8,128)(2,1)} %fusion.84, bf16[1024,256]{1,0:T(8,128)(2,1)S(1)} %bitcast.172, f32[64,16]{1,0:T(8,128)S(1)} %bitcast.180), kind=kOutput, calls=%fused_computation.23.clone.1 | convolution fusion | flops 268566528 | bytes 2916352 | tf_op jit(solution)/shard_map/while/body/eval_jaxpr/tgjk,gkd->tgjd/dot_general | solution.py:52
  171.4 1.6 fusion.86
  173.5 2.7 fusion.88
  176.3 1.6 fusion.89
  179.4 2.8 fusion.92
  188.5 1.1 fusion.83
  189.6 2.1 fusion.84
  192.7 3.7 %fusion.85 = f32[1,128,64,16]{1,3,2,0:T(8,128)} fusion(bf16[64,16,1024]{2,0,1:T(8,128)(2,1)} %fusion.84, bf16[1024,256]{1,0:T(8,128)(2,1)S(1)} %bitcast.172, f32[64,16]{1,0:T(8,128)S(1)} %bitcast.180), kind=kOutput, calls=%fused_computation.23.clone.1 | convolution fusion | flops 268566528 | bytes 2916352 | tf_op jit(solution)/shard_map/while/body/eval_jaxpr/tgjk,gkd->tgjd/dot_general | solution.py:52
  196.5 1.6 fusion.86
  198.5 2.7 fusion.88
  201.3 1.6 fusion.89
  204.5 2.8 fusion.92
  213.5 1.1 fusion.83
  214.6 2.1 fusion.84
  217.8 3.7 %fusion.85 = f32[1,128,64,16]{1,3,2,0:T(8,128)} fusion(bf16[64,16,1024]{2,0,1:T(8,128)(2,1)} %fusion.84, bf16[1024,256]{1,0:T(8,128)(2,1)S(1)} %bitcast.172, f32[64,16]{1,0:T(8,128)S(1)} %bitcast.180), kind=kOutput, calls=%fused_computation.23.clone.1 | convolution fusion | flops 268566528 | bytes 2916352 | tf_op jit(solution)/shard_map/while/body/eval_jaxpr/tgjk,gkd->tgjd/dot_general | solution.py:52
  221.6 1.6 fusion.86
  223.6 2.7 fusion.88
  226.4 1.6 fusion.89
  229.5 2.8 fusion.92
  238.6 1.1 fusion.83
  239.7 2.1 fusion.84
  242.8 3.7 %fusion.85 = f32[1,128,64,16]{1,3,2,0:T(8,128)} fusion(bf16[64,16,1024]{2,0,1:T(8,128)(2,1)} %fusion.84, bf16[1024,256]{1,0:T(8,128)(2,1)S(1)} %bitcast.172, f32[64,16]{1,0:T(8,128)S(1)} %bitcast.180), kind=kOutput, calls=%fused_computation.23.clone.1 | convolution fusion | flops 268566528 | bytes 2916352 | tf_op jit(solution)/shard_map/while/body/eval_jaxpr/tgjk,gkd->tgjd/dot_general | solution.py:52
  246.6 1.6 fusion.86
  248.7 2.7 fusion.88
  251.5 1.6 fusion.89
  254.6 2.8 fusion.92
  264.8 2.1 fusion.84
  267.9 3.7 %fusion.85 = f32[1,128,64,16]{1,3,2,0:T(8,128)} fusion(bf16[64,16,1024]{2,0,1:T(8,128)(2,1)} %fusion.84, bf16[1024,256]{1,0:T(8,128)(2,1)S(1)} %bitcast.172, f32[64,16]{1,0:T(8,128)S(1)} %bitcast.180), kind=kOutput, calls=%fused_computation.23.clone.1 | convolution fusion | flops 268566528 | bytes 2916352 | tf_op jit(solution)/shard_map/while/body/eval_jaxpr/tgjk,gkd->tgjd/dot_general | solution.py:52
  271.7 1.6 fusion.86
  273.7 2.7 fusion.88
  276.5 1.6 fusion.89
  279.7 2.8 fusion.92
  (217 shorter events, 61.6 us)
Async XLA Ops:
  7.4 1.5 copy-start
  7.4 4.2 %copy-start.2 = (bf16[512,1,128]{2,0,1:T(8,128)(2,1)S(1)}, bf16[512,1,128]{2,0,1:T(8,128)(2,1)}, u32[]{:S(2)}) copy-start(bf16[512,1,128]{2,0,1:T(8,128)(2,1)} %param.13) | copy-start | bytes 393220
  7.4 4.2 %copy-start.3 = (bf16[512,1,128]{2,0,1:T(8,128)(2,1)S(1)}, bf16[512,1,128]{2,0,1:T(8,128)(2,1)}, u32[]{:S(2)}) copy-start(bf16[512,1,128]{2,0,1:T(8,128)(2,1)} %param.14) | copy-start | bytes 393220
  7.4 10.0 %copy-start.6 = (s32[8,1,16]{2,1,0:T(1,128)S(1)}, s32[8,1,16]{2,1,0:T(1,128)}, u32[]{:S(2)}) copy-start(s32[8,1,16]{2,1,0:T(1,128)} %param.17) | copy-start | bytes 1540
  7.4 10.1 %copy-start.4 = (f32[64,128]{1,0:T(8,128)S(1)}, f32[64,128]{1,0:T(8,128)}, u32[]{:S(2)}) copy-start(f32[64,128]{1,0:T(8,128)} %param.16) | copy-start | bytes 98308
  7.4 10.1 %copy-start.5 = (f32[64,128]{1,0:T(8,128)S(1)}, f32[64,128]{1,0:T(8,128)}, u32[]{:S(2)}) copy-start(f32[64,128]{1,0:T(8,128)} %param.15) | copy-start | bytes 98308
  7.4 38.1 %reduce-scatter.2.cloned.1.call-start = ((), (), s32[]{:S(2)}) async-start(), calls=%async_computation.1 | async-start | bytes 491520 | tf_op jit(solution)/shard_map/reduce_scatter | solution.py:74
  11.5 59.7 %all-gather.2.cloned.1.call-start = ((), (), s32[]{:S(2)}) async-start(), calls=%async_computation.2 | async-start | bytes 8650752 | tf_op jit(solution)/shard_map/all_gather | solution.py:88
  11.7 0.7 copy-start.1
  12.4 31.3 %collective-permute-start = (bf16[512,256]{1,0:T(8,128)(2,1)}, bf16[512,256]{1,0:T(8,128)(2,1)S(1)}, u32[]{:S(2)}, u32[]{:S(2)}) collective-permute-start(bf16[512,256]{1,0:T(8,128)(2,1)} %bitcast.175), channel_id=1, source_target_pairs={{0,4},{4,8},{8,12},{12,16},{16,20},{20,24},{24,28},{28,32},{32,36}... | collective-permute-start | bytes 786440 | tf_op jit(solution)/shard_map/ppermute | solution.py:12
Sparse Core Ops, SparseCore 0:
  11.6 22.3 reduce-scatter.1
Sparse Core Ops, SparseCore 1:
  14.5 56.6 all-gather.1
where the time goes:
time: 293 us; the launch traced here: 290 us
  matrix products  108 us (37%)
  other arithmetic  51.1 us (17%)
  local copies, waits for them, and re-layouts  41.5 us (14%)
  blocking collectives  24.4 us (8%)
  waiting for transfers between devices  24.1 us (8%)
  loops' own time  20.8 us (7%)
  between operations  15 us (5%)
  starting transfers between devices  5.02 us (2%)
    dot_general x16, matrix products, attend(): jnp.einsum('tgjk,gkd->tgjd', rounded, value_rows, preferred_element_type=...  51.4 us
    all_gather x1, blocking collectives, body(): summaries = lax.all_gather(summary, 'ctx', axis=0, tiled=True)  24.4 us
    all_gather x1, waiting for transfers between devices, body(): all_blocks = lax.all_gather(blocks, 'ctx', axis=0, tiled=True)  24 us
    another operation x16, other arithmetic  21.9 us
    dot_general x8, matrix products, attend(): jnp.einsum('tgjk,gkd->tgjd', rounded.astype(jnp.float32), value_rows, pre...  21.3 us
    another operation x1, loops' own time, body(): results = lax.map(per_block, jnp.arange(blocks_here, dtype=jnp.int32))  20.8 us
    dot_general x16, matrix products, attend(): jnp.einsum('tgjd,gkd->tgjk', query_block_index, key_rows, preferred_eleme...  20 us
    reduce_sum x24, other arithmetic, attend(): total_w = jnp.sum(weights, axis=-1, keepdims=True)  17.6 us
  transfers between devices with their start and end apart: 3, of which 1 were waited for; matrix products, arithmetic and copies ran while one was open for 2% of the time, Pallas kernels for 0%

commit v1 on v0

--- a/solution.py
+++ b/solution.py
@@ -2,6 +2,7 @@
 import jax.numpy as jnp
 from jax import lax
 from jax.sharding import PartitionSpec as P
+from jax.lax import all_to_all, psum
 
 WINDOW_TOKENS = 512
 
@@ -85,7 +86,12 @@
     blocks = key_value.reshape(blocks_here, block_len, 2 * head_dim)
     chosen_blocks = selection[:, 0, :]
     all_ids = jnp.arange(block_count_total, dtype=jnp.int32)
-    all_blocks = lax.all_gather(blocks, "ctx", axis=0, tiled=True)
+    sheets = []
+    for _ in range(psum(1, axis_name="ctx")):
+        sheets.append(blocks)
+    all_blocks = jnp.concatenate(
+        all_to_all(jnp.stack(sheets, axis=0), axis_name="ctx", split_axis=0, concat_axis=0), axis=0
+    )
     picked = jnp.take(all_blocks, chosen_blocks, axis=0)
     offset = own_index * rows_here
     comp_ends = (all_ids + 1) * block_len - 1

time: 293 us -> 378 us (1.29)
  blocking collectives: 24.4 us -> 134 us
  waiting for transfers between devices: 24.1 us -> 0.04 us
  matrix products: 108 us -> 95.3 us
  starting transfers between devices: 5.02 us -> 13.2 us
  other arithmetic: 51.1 us -> 57.2 us
    all_gather x1, blocking collectives: 24.4 us -> 134 us  [body(): summaries = lax.all_gather(summary, 'ctx', axis=0, tiled=True)]
    all_gather x1 -> x0, waiting for transfers between devices: 24 us -> none  [body(): all_blocks = lax.all_gather(blocks, 'ctx', axis=0, tiled=True)]
    all_to_all x0 -> x1, starting transfers between devices: none -> 9.62 us  [body(): all_to_all(jnp.stack(sheets, axis=0), axis_name='ctx', split_axis=0, conc...]
    another operation x16, other arithmetic: 21.9 us -> 30.6 us
    dot_general x8, matrix products: 12.6 us -> 5.34 us  [attend(): jnp.einsum('tgjd,gkd->tgjk', query_block_index.astype(jnp.float32), key_r...]
    dot_general x16, matrix products: 20 us -> 12.7 us  [attend(): jnp.einsum('tgjd,gkd->tgjk', query_block_index, key_rows, preferred_eleme...]
    slice x8, local copies, waits for them, and re-layouts: 7.86 us -> 0.93 us  [per_block(): gate_block_rows[..., 2:3] * out_win]
    another operation x0 -> x1, local copies, waits for them, and re-layouts: none -> 4.28 us  [body(): jnp.stack(sheets, axis=0)]
  transfers between devices with their start and end apart: 3 -> 3, of which waited for: 1 -> 0; matrix products, arithmetic and copies ran while one was open for 2% -> 1% of each run, Pallas kernels for 0% -> 0%
where the time goes in v1:
time: 378 us; the launch traced here: 374 us
  blocking collectives  134 us (35%)
  matrix products  95.3 us (25%)
  other arithmetic  57.2 us (15%)
  local copies, waits for them, and re-layouts  38.5 us (10%)
  loops' own time  22.9 us (6%)
  between operations  13.6 us (4%)
  starting transfers between devices  13.2 us (3%)
    all_gather x1, blocking collectives, body(): summaries = lax.all_gather(summary, 'ctx', axis=0, tiled=True)  134 us
    dot_general x16, matrix products, attend(): jnp.einsum('tgjk,gkd->tgjd', rounded, value_rows, preferred_element_type=...  54.8 us
    another operation x16, other arithmetic  30.6 us
    another operation x1, loops' own time, body(): results = lax.map(per_block, jnp.arange(blocks_here, dtype=jnp.int32))  22.9 us
    dot_general x8, matrix products, attend(): jnp.einsum('tgjk,gkd->tgjd', rounded.astype(jnp.float32), value_rows, pre...  21 us
    reduce_sum x24, other arithmetic, attend(): total_w = jnp.sum(weights, axis=-1, keepdims=True)  17.6 us
    dot_general x16, matrix products, attend(): jnp.einsum('tgjd,gkd->tgjk', query_block_index, key_rows, preferred_eleme...  12.7 us
    all_to_all x1, starting transfers between devices, body(): all_to_all(jnp.stack(sheets, axis=0), axis_name='ctx', split_axis=0, conc...  9.62 us
  transfers between devices with their start and end apart: 3, of which 0 were waited for; matrix products, arithmetic and copies ran while one was open for 1% of the time, Pallas kernels for 0%

profile of v1, /device:TPU:1, one launch (start us, length us, event | category | flops | bytes accessed | tf_op | source)
XLA Modules:
  0.0 374.4 jit_solution(9893987944380831838)
XLA Ops:
  8.5 4.3 %stack.3 = bf16[32,8,64,256]{3,2,1,0:T(8,128)(2,1)} broadcast(bf16[8,64,256]{2,1,0:T(8,128)(2,1)S(1)} %bitcast.175), dimensions={1,2,3} | broadcast | bytes 8650752 | tf_op jit(solution)/shard_map/stack | solution.py:93
  12.8 9.6 %all-to-all-start = ((bf16[32,8,64,256]{3,2,1,0:T(8,128)(2,1)}), bf16[32,8,64,256]{3,2,1,0:T(8,128)(2,1)}, u32[]{:S(2)}, u32[]{:S(2)}) async-start(bf16[32,8,64,256]{3,2,1,0:T(8,128)(2,1)} %stack.3), calls=%async_computation.1 | async-start | bytes 16777216 | tf_op jit(solution)/shard_map/all_to_all | solution.py:93
  22.5 3.5 collective-permute-start
  26.1 1.5 fusion.55
  27.8 133.7 %all_gather.3 = f32[256,256]{1,0:T(8,128)S(1)} all-gather(f32[8,256]{1,0:T(8,128)S(1)} %multiply_reduce_fusion), channel_id=1, replica_groups=mesh['ctx'=32,'head'=4] {'ctx'}, dimensions={0}, use_global_device_ids=true | all-gather | bytes 270336 | tf_op jit(solution)/shard_map/all_gather | solution.py:83
  162.6 6.2 %gather_fusion = bf16[128,64,256]{2,1,0:T(8,128)(2,1)} fusion(bf16[256,64,256]{2,1,0:T(8,128)(2,1)} %bitcast.4, s32[1024]{0:T(1024)S(1)} %pad_clamp_fusion), kind=kCustom, calls=%fused_computation | custom fusion | bytes 8389120 | tf_op jit(solution)/shard_map/jit(_take)/gather | solution.py:95
  168.8 4.6 %broadcast_select_fusion = bf16[8,16,64,256]{3,2,1,0:T(8,128)(2,1)} fusion(bf16[8,16,64,256]{3,2,1,0:T(8,128)(2,1)} %bitcast.174, pred[8,16]{1,0:T(8,128)(4,1)S(1)} %compare_and_fusion), kind=kLoop, calls=%fused_computation.68 | loop fusion | flops 2097152 | bytes 8388736 | tf_op jit(solution)/shard_map/jit(_take)/select_n | solution.py:95
  173.3 194.2 %while.15 = (s32[]{:T(128)}, bf16[8,64,16,128]{3,2,1,0:T(8,128)(2,1)}, s32[8]{0:T(128)S(1)}, f32[512,1,16,3]{0,3,2,1:T(4,128)S(1)}, s32[]{:T(128)}, /*index=5*/b...) while((s32[]{:T(128)}, ...), condition=%wide.region_9.10_spmd.clone.clone, body=%wide.region_2.9_spmd.clone.clone.sunk | while | flops 1666942592 | bytes 40133232 | solution.py:147
  177.4 1.8 fusion.91
  181.4 1.1 constant_dynamic-slice_fusion.10
  183.4 1.1 fusion.83
  184.5 2.1 fusion.84
  186.8 3.7 fusion.85
  191.7 2.6 fusion.88
  194.4 3.1 fusion.92
  201.7 1.8 fusion.91
  205.7 1.1 constant_dynamic-slice_fusion.10
  207.7 1.1 fusion.83
  208.8 2.1 fusion.84
  211.1 3.7 fusion.85
  216.0 2.6 fusion.88
  218.7 3.1 fusion.92
  225.9 1.8 fusion.91
  230.0 1.1 constant_dynamic-slice_fusion.10
  232.0 1.1 fusion.83
  233.1 2.1 fusion.84
  235.3 3.7 fusion.85
  240.3 2.6 fusion.88
  243.0 3.1 fusion.92
  250.2 1.8 fusion.91
  254.3 1.1 constant_dynamic-slice_fusion.10
  256.2 1.1 fusion.83
  257.3 2.1 fusion.84
  259.6 3.7 fusion.85
  264.6 2.6 fusion.88
  267.3 3.1 fusion.92
  274.5 1.8 fusion.91
  278.6 1.1 constant_dynamic-slice_fusion.10
  280.5 1.1 fusion.83
  281.6 2.1 fusion.84
  283.9 3.7 fusion.85
  288.9 2.6 fusion.88
  291.6 3.1 fusion.92
  298.8 1.8 fusion.91
  302.8 1.1 constant_dynamic-slice_fusion.10
  304.8 1.1 fusion.83
  305.9 2.1 fusion.84
  308.2 3.7 fusion.85
  313.1 2.6 fusion.88
  315.9 3.1 fusion.92
  323.1 1.8 fusion.91
  327.1 1.1 constant_dynamic-slice_fusion.10
  329.1 1.1 fusion.83
  330.2 2.1 fusion.84
  332.5 3.7 fusion.85
  337.4 2.6 fusion.88
  340.1 3.1 fusion.92
  347.3 1.8 fusion.91
  351.4 1.1 constant_dynamic-slice_fusion.10
  353.4 1.1 fusion.83
  354.5 2.1 fusion.84
  356.7 3.7 fusion.85
  361.7 2.6 fusion.88
  364.4 3.1 fusion.92
  (293 shorter events, 50.8 us)
Async XLA Ops:
  6.5 19.5 %copy-start = (bf16[512,1792]{1,0:T(8,128)(2,1)S(1)}, bf16[512,1792]{1,0:T(8,128)(2,1)}, u32[]{:S(2)}) copy-start(bf16[512,1792]{1,0:T(8,128)(2,1)} %param.10) | copy-start | bytes 5505028
  12.8 13.3 %copy-start.3 = (bf16[1792,192]{0,1:T(8,128)(2,1)S(1)}, bf16[1792,192]{0,1:T(8,128)(2,1)}, u32[]{:S(2)}) copy-start(bf16[1792,192]{0,1:T(8,128)(2,1)} %param.11) | copy-start | bytes 2064388
  12.8 149.8 %all-to-all-start = ((bf16[32,8,64,256]{3,2,1,0:T(8,128)(2,1)}), bf16[32,8,64,256]{3,2,1,0:T(8,128)(2,1)}, u32[]{:S(2)}, u32[]{:S(2)}) async-start(bf16[32,8,64,256]{3,2,1,0:T(8,128)(2,1)} %stack.3), calls=%async_computation.1 | async-start | bytes 16777216 | tf_op jit(solution)/shard_map/all_to_all | solution.py:93
  22.4 5.2 %copy-start.6 = (s32[8,1,16]{2,1,0:T(1,128)S(1)}, s32[8,1,16]{2,1,0:T(1,128)}, u32[]{:S(2)}) copy-start(s32[8,1,16]{2,1,0:T(1,128)} %param.17) | copy-start | bytes 1540
  22.5 5.3 %copy-start.4 = (f32[64,128]{1,0:T(8,128)S(1)}, f32[64,128]{1,0:T(8,128)}, u32[]{:S(2)}) copy-start(f32[64,128]{1,0:T(8,128)} %param.16) | copy-start | bytes 98308
  22.5 5.2 %copy-start.5 = (f32[64,128]{1,0:T(8,128)S(1)}, f32[64,128]{1,0:T(8,128)}, u32[]{:S(2)}) copy-start(f32[64,128]{1,0:T(8,128)} %param.15) | copy-start | bytes 98308
  22.5 139.1 %reduce-scatter.2.cloned.1.call-start = ((), (), s32[]{:S(2)}) async-start(), calls=%async_computation.2 | async-start | bytes 491520 | tf_op jit(solution)/shard_map/reduce_scatter | solution.py:75
  22.5 139.0 %collective-permute-start = (bf16[512,256]{1,0:T(8,128)(2,1)S(1)}, bf16[512,256]{1,0:T(8,128)(2,1)S(1)}, u32[]{:S(2)}, u32[]{:S(2)}) collective-permute-start(bf16[512,256]{1,0:T(8,128)(2,1)S(1)} %bitcast.176), channel_id=1, source_target_pairs={{0,4},{4,8},{8,12},{12,16},{16,20},{20,24},{24,28},{28,32},{32,36}... | collective-permute-start | bytes 786440 | tf_op jit(solution)/shard_map/ppermute | solution.py:13
  173.3 1.4 copy-start.8
  173.4 4.0 %copy-start.1 = (bf16[1024,256]{1,0:T(8,128)(2,1)}, bf16[1024,256]{1,0:T(8,128)(2,1)S(1)}, u32[]{:S(2)}) copy-start(bf16[1024,256]{1,0:T(8,128)(2,1)S(1)} %get-tuple-element.455) | copy-start | bytes 1572868 | tf_op jit(solution)/shard_map/while
  194.4 3.2 copy-start.2
  194.4 3.2 copy-start.7
  194.4 3.2 copy-start.9
  197.6 1.4 copy-start.8
  197.6 4.0 %copy-start.1 = (bf16[1024,256]{1,0:T(8,128)(2,1)}, bf16[1024,256]{1,0:T(8,128)(2,1)S(1)}, u32[]{:S(2)}) copy-start(bf16[1024,256]{1,0:T(8,128)(2,1)S(1)} %get-tuple-element.455) | copy-start | bytes 1572868 | tf_op jit(solution)/shard_map/while
  218.6 3.2 copy-start.2
  218.6 3.2 copy-start.7
  218.6 3.2 copy-start.9
  221.9 1.4 copy-start.8
  221.9 4.0 %copy-start.1 = (bf16[1024,256]{1,0:T(8,128)(2,1)}, bf16[1024,256]{1,0:T(8,128)(2,1)S(1)}, u32[]{:S(2)}) copy-start(bf16[1024,256]{1,0:T(8,128)(2,1)S(1)} %get-tuple-element.455) | copy-start | bytes 1572868 | tf_op jit(solution)/shard_map/while
  242.9 3.2 copy-start.2
  242.9 3.2 copy-start.7
  242.9 3.2 copy-start.9
  246.2 1.4 copy-start.8
  246.2 4.0 %copy-start.1 = (bf16[1024,256]{1,0:T(8,128)(2,1)}, bf16[1024,256]{1,0:T(8,128)(2,1)S(1)}, u32[]{:S(2)}) copy-start(bf16[1024,256]{1,0:T(8,128)(2,1)S(1)} %get-tuple-element.455) | copy-start | bytes 1572868 | tf_op jit(solution)/shard_map/while
  267.2 3.2 copy-start.2
  267.2 3.2 copy-start.7
  267.2 3.2 copy-start.9
  270.4 1.4 copy-start.8
  270.5 4.0 %copy-start.1 = (bf16[1024,256]{1,0:T(8,128)(2,1)}, bf16[1024,256]{1,0:T(8,128)(2,1)S(1)}, u32[]{:S(2)}) copy-start(bf16[1024,256]{1,0:T(8,128)(2,1)S(1)} %get-tuple-element.455) | copy-start | bytes 1572868 | tf_op jit(solution)/shard_map/while
  291.5 3.2 copy-start.2
  291.5 3.2 copy-start.7
  291.5 3.2 copy-start.9
  294.7 1.4 copy-start.8
  294.7 4.0 %copy-start.1 = (bf16[1024,256]{1,0:T(8,128)(2,1)}, bf16[1024,256]{1,0:T(8,128)(2,1)S(1)}, u32[]{:S(2)}) copy-start(bf16[1024,256]{1,0:T(8,128)(2,1)S(1)} %get-tuple-element.455) | copy-start | bytes 1572868 | tf_op jit(solution)/shard_map/while
  315.8 3.2 copy-start.2
  315.8 3.2 copy-start.7
  315.8 3.2 copy-start.9
  319.0 1.4 copy-start.8
  319.0 4.0 %copy-start.1 = (bf16[1024,256]{1,0:T(8,128)(2,1)}, bf16[1024,256]{1,0:T(8,128)(2,1)S(1)}, u32[]{:S(2)}) copy-start(bf16[1024,256]{1,0:T(8,128)(2,1)S(1)} %get-tuple-element.455) | copy-start | bytes 1572868 | tf_op jit(solution)/shard_map/while
  340.0 3.2 copy-start.2
  340.0 3.2 copy-start.7
  340.0 3.2 copy-start.9
  343.3 1.4 copy-start.8
  343.3 4.0 %copy-start.1 = (bf16[1024,256]{1,0:T(8,128)(2,1)}, bf16[1024,256]{1,0:T(8,128)(2,1)S(1)}, u32[]{:S(2)}) copy-start(bf16[1024,256]{1,0:T(8,128)(2,1)S(1)} %get-tuple-element.455) | copy-start | bytes 1572868 | tf_op jit(solution)/shard_map/while
  364.3 3.2 copy-start.2
  364.3 3.2 copy-start.7
  364.3 3.2 copy-start.9
Sparse Core Ops, SparseCore 0:
  27.7 19.9 reduce-scatter.1
